TPU v7x, 256 devices: a whole 4x4x8 slice. The times are simulated.
256 devices in a mesh: req: 64 (over y, z_hi, x, core), dec: 4 (over z_lo).
Axes of the slice: x: 4, y: 4, z: 8 (z_hi: 2, z_lo: 4; z = z_hi * 4 + z_lo), core: 2. Of those that a mesh axis runs over, the one named last changes fastest.
Arguments:
- queries: bfloat16 [32768, 2048], P('req', 'dec')
- keys: bfloat16 [32768, 2048], P('req', 'dec'), may hold values from -6 to 6
- values: bfloat16 [32768, 2048], P('req', 'dec'), may hold values from -6 to 6
- resid: bfloat16 [32768, 2048], P('req', 'dec'), may hold values from -6 to 6
- seg_ids: int32 [32768], P('req'), may hold values from -1 to 7, as said below
- out_weight: bfloat16 [2048, 2048], P('dec'), may hold values from -0.125 to 0.125
- norm_gain: float32 [2048], replicated, may hold values from 0.1 to 1.9
- adapter_down: bfloat16 [2048, 128], replicated, may hold values from -0.125 to 0.125
- adapter_up: bfloat16 [128, 4096], P(None, ('req', 'dec')), may hold values from -0.5 to 0.5
- gate_weight: bfloat16 [2048, 4096], P(None, ('req', 'dec')), may hold values from -0.125 to 0.125
- up_weight: bfloat16 [2048, 4096], P(None, ('req', 'dec')), may hold values from -0.125 to 0.125
- down_weight: bfloat16 [4096, 2048], P(('req', 'dec')), may hold values from -0.09375 to 0.09375
- row_order: int32 [64, 512], P('req'), may hold values from 0 to 511, each once within a row
- block_table: int32 [64, 8], P('req'), may hold values from 0 to 7, each once within a row
Outputs:
- block_out: bfloat16 [32768, 2048], P('req', 'dec')
- kv_cache: bfloat16 [512, 64, 4096], P(('req', 'dec'))
Inputs may be any that keep to these rules, and one draw needn't show every extreme that they name: `seg_ids`: within each index of req the live slots come first, grouped into requests whose numbers start at 0, rise by one from request to request and never fall, then come padding slots marked -1; some index of req holds one request that fills all its 512 slots, and when there is more than one index of req, some other index holds request numbers up to the stated most.
All inputs are finite; a program needn't handle non-finite values.
Results may differ from a plain program's by a relative error of at most 0.017.
Values may be sent and summed in bfloat16 or wider, within the bound.
A program may use at most 128 MiB of HBM per device.

v0:
```python
import jax
import jax.numpy as jnp
from jax import lax
from jax.sharding import PartitionSpec as P

HD = 128


def attend(query_rows, key_rows, value_rows, segment):
    row_count = query_rows.shape[0]
    head_count = query_rows.shape[1] // HD
    query_heads = query_rows.reshape(row_count, head_count, HD)
    key_heads = key_rows.reshape(row_count, head_count, HD)
    value_heads = value_rows.reshape(row_count, head_count, HD)
    scores = jnp.einsum(
        "qhd,khd->hqk", query_heads, key_heads, preferred_element_type=jnp.float32
    ) * HD ** (-0.5)
    position = jnp.arange(row_count)
    allowed = (
        (segment[:, None] == segment[None, :])
        & (position[None, :] <= position[:, None])
        & (segment[:, None] >= 0)
    )
    masked = jnp.where(allowed[None], scores, -1e30)
    highest = jnp.max(masked, axis=-1, keepdims=True)
    exponent = jnp.where(allowed[None], jnp.exp(masked - highest), 0.0)
    denominator = jnp.sum(exponent, axis=-1, keepdims=True)
    denominator = jnp.where(denominator > 0, denominator, 1.0)
    weights = (exponent / denominator).astype(jnp.bfloat16)
    result = jnp.einsum("hqk,khd->qhd", weights, value_heads, preferred_element_type=jnp.float32)
    return result.astype(jnp.bfloat16).reshape(row_count, head_count * HD)


def body(
    queries,
    keys,
    values,
    resid,
    seg_ids,
    out_weight,
    norm_gain,
    adapter_down,
    adapter_up,
    gate_weight,
    up_weight,
    down_weight,
    row_order,
    block_table,
):
    slot_count = queries.shape[0]
    features = keys.shape[1]
    block_count = block_table.shape[1]
    block_slots = slot_count // block_count
    table_row = block_table[0]
    placement = (jnp.arange(block_count)[:, None] == table_row[None, :]).astype(jnp.bfloat16)
    key_blocks = keys.reshape(block_count, block_slots, features)
    value_blocks = values.reshape(block_count, block_slots, features)
    ordered_keys = jnp.einsum(
        "tj,jbw->tbw", placement, key_blocks, preferred_element_type=jnp.float32
    ).astype(jnp.bfloat16)
    ordered_values = jnp.einsum(
        "tj,jbw->tbw", placement, value_blocks, preferred_element_type=jnp.float32
    ).astype(jnp.bfloat16)
    moved_keys, moved_values = (
        lax.all_to_all(ordered_keys, "dec", split_axis=0, concat_axis=2, tiled=True),
        lax.all_to_all(ordered_values, "dec", split_axis=0, concat_axis=2, tiled=True),
    )
    kv_cache = jnp.concatenate([moved_keys, moved_values], axis=2)
    attn = attend(queries, keys, values, seg_ids)
    partial_value = jnp.dot(attn, out_weight, preferred_element_type=jnp.float32).astype(
        jnp.bfloat16
    )
    head_total = lax.psum_scatter(partial_value, "dec", scatter_dimension=1, tiled=True).astype(
        jnp.float32
    )
    hidden = (resid.astype(jnp.float32) + head_total).astype(jnp.bfloat16)
    permuted = jnp.take(hidden, row_order[0], axis=0)
    whole_rows = lax.all_gather(permuted, "dec", axis=1, tiled=True)
    mixed_rows = lax.all_to_all(whole_rows, "req", split_axis=0, concat_axis=0, tiled=True)
    quarter = resid.shape[1]
    column = lax.dynamic_slice_in_dim(mixed_rows, lax.axis_index("dec") * quarter, quarter, 1)
    values_f = mixed_rows.astype(jnp.float32)
    scale = lax.rsqrt(jnp.mean(values_f * values_f, axis=-1, keepdims=True) + 1e-05)
    normed = (values_f * scale * norm_gain).astype(jnp.bfloat16)
    low_rank = jnp.dot(normed, adapter_down, preferred_element_type=jnp.float32).astype(
        jnp.bfloat16
    )
    operand = jnp.concatenate([normed, low_rank], axis=1)
    rank_width = adapter_down.shape[1]
    piece_width = gate_weight.shape[1]
    padding = jnp.zeros((rank_width, piece_width), jnp.bfloat16)
    stacked = jnp.stack(
        [
            jnp.concatenate([gate_weight, adapter_up], axis=0),
            jnp.concatenate([up_weight, padding], axis=0),
        ]
    )
    projected = jnp.einsum(
        "md,gdc->gmc",
        operand,
        lax.all_gather(stacked, "req", axis=2, tiled=True),
        preferred_element_type=jnp.float32,
    )
    hidden_units = (jax.nn.gelu(projected[0]) * projected[1]).astype(jnp.bfloat16)
    down_full = lax.all_gather(down_weight, "req", axis=0, tiled=True)
    down_part = jnp.dot(hidden_units, down_full, preferred_element_type=jnp.float32).astype(
        jnp.bfloat16
    )
    mlp_total = lax.psum_scatter(down_part, "dec", scatter_dimension=1, tiled=True).astype(
        jnp.float32
    )
    block_out = (column.astype(jnp.float32) + mlp_total).astype(jnp.bfloat16)
    return (block_out, kv_cache)


def solution(mesh):
    placed = (
        P("req", "dec"),
        P("req", "dec"),
        P("req", "dec"),
        P("req", "dec"),
        P("req"),
        P("dec", None),
        P(),
        P(),
        P(None, ("req", "dec")),
        P(None, ("req", "dec")),
        P(None, ("req", "dec")),
        P(("req", "dec"), None),
        P("req", None),
        P("req", None),
    )
    return jax.shard_map(
        body,
        mesh=mesh,
        in_specs=placed,
        out_specs=(P("req", "dec"), P(("req", "dec"), None, None)),
        check_vma=False,
    )
```

profile of v0, /device:TPU:1, one launch (start us, length us, event | category | flops | bytes accessed | tf_op | source)
XLA Modules:
  0.0 435.6 jit_solution(6591187465169870902)
XLA Ops:
  7.2 0.0 copy-start
  7.2 0.0 reduce-scatter.3.cloned.1.call-start
  7.2 0.8 broadcast_compare_fusion
  8.1 1.0 fusion.26
  9.0 1.9 fusion.27
  11.0 4.1 fusion.46
  15.1 0.2 copy.44
  15.3 2.6 fusion.19
  18.0 2.6 convolution_convert_fusion.1
  20.6 0.0 reduce-scatter.3.cloned.1.call-update
  20.7 0.0 copy-start.12
  20.7 0.0 all-gather.4.cloned.1.call-start
  20.8 52.3 %reduce-scatter.3.cloned.1.call-done = bf16[512,512]{1,0:T(8,128)(2,1)} async-done(((bf16[512,2048]{1,0:T(8,128)(2,1)}), bf16[512,512]{1,0:T(8,128)(2,1)}) %reduce-scatter.3.cloned.1.call-update) | async-done | bytes 524304 | tf_op jit(solution)/shard_map/reduce_scatter | solution.py:73
  73.1 1.2 add_convert_fusion.1
  74.3 2.0 gather_fusion
  76.2 0.9 broadcast_select_fusion
  77.2 0.0 all-gather.4.cloned.1.call-update
  77.2 0.0 all-gather.6.cloned.1.call-start
  77.3 0.7 pad_maximum_fusion.1
  78.0 0.0 all-gather.6.cloned.1.call-update
  78.0 0.0 all-gather.8.cloned.1.call-start
  78.1 0.5 all-gather.8.cloned.1.call-update
  78.6 0.0 reduce-scatter.5.cloned.1.call-start
  78.6 48.0 %all-gather.4.cloned.1.call-done = bf16[512,2048]{1,0:T(8,128)(2,1)} async-done(((bf16[512,512]{1,0:T(8,128)(2,1)}), bf16[512,2048]{1,0:T(8,128)(2,1)}) %all-gather.4.cloned.1.call-update) | async-done | bytes 2097168 | tf_op jit(solution)/shard_map/all_gather | solution.py:78
  126.7 62.3 %all_to_all.48 = bf16[64,8,2048]{2,1,0:T(8,128)(2,1)S(1)} all-to-all(bf16[64,8,2048]{2,1,0:T(8,128)(2,1)} %bitcast.72), channel_id=1, replica_groups=mesh['req'=64,'dec'=4] {'req'}, dimensions={0} | all-to-all | bytes 4194304 | tf_op jit(solution)/shard_map/all_to_all | solution.py:79
  188.9 1.3 copy-done.1
  190.3 0.5 multiply_reduce_fusion
  190.8 0.1 rsqrt.12
  190.9 2.1 multiply_convert_fusion
  193.0 1.3 copy-done.2
  194.3 0.8 convolution_convert_fusion.4
  195.2 0.1 copy.36
  195.3 70.0 %all-gather.6.cloned.1.call-done = bf16[2,2176,1024]{1,2,0:T(8,128)(2,1)} async-done(((bf16[2,2176,16]{1,2,0:T(8,128)(2,1)}), bf16[2,2176,1024]{1,2,0:T(8,128)(2,1)}) %all-gather.6.cloned.1.call-update) | async-done | bytes 8912912 | tf_op jit(solution)/shard_map/all_gather | solution.py:101
  265.3 10.6 %fusion.5 = f32[2,512,1024]{1,2,0:T(8,128)} fusion(bf16[2,2176,1024]{1,2,0:T(8,128)(2,1)} %all-gather.6.cloned.1.call-done, bf16[512,128]{1,0:T(8,128)(2,1)S(1)} %copy.36, bf16[512,2048]{1,0:T(8,128)(2,1)} %copy-done.2), kind=kOutput, calls=%fused_computation.15 | convolution fusion | flops 4567859200 | bytes 15335424 | tf_op jit(solution)/shard_map/md,gdc->gmc/dot_general | solution.py:98
  275.9 79.1 %all-gather.8.cloned.1.call-done = bf16[1024,2048]{1,0:T(8,128)(2,1)} async-done(((bf16[16,2048]{1,0:T(8,128)(2,1)}), bf16[1024,2048]{1,0:T(8,128)(2,1)}) %all-gather.8.cloned.1.call-update) | async-done | bytes 4194320 | tf_op jit(solution)/shard_map/all_gather | solution.py:105
  355.0 7.4 %convolution_convert_fusion = bf16[512,2048]{1,0:T(8,128)(2,1)} fusion(bf16[1024,2048]{1,0:T(8,128)(2,1)} %all-gather.8.cloned.1.call-done, f32[2,512,1024]{1,2,0:T(8,128)} %fusion.5), kind=kOutput, calls=%fused_computation.9 | convolution fusion | flops 2153775104 | bytes 10485760 | tf_op jit(solution)/shard_map/dot_general | solution.py:106
  362.3 0.0 reduce-scatter.5.cloned.1.call-update
  362.4 0.4 convolution_convert_fusion.3
  362.8 0.9 copy.38
  363.7 3.5 all-to-all-start.1
  367.2 0.4 convolution_convert_fusion.2
  367.6 0.9 copy.41
  368.6 27.2 %all-to-all-done.1 = bf16[8,64,512]{2,1,0:T(8,128)(2,1)S(1)} async-done(((bf16[8,64,512]{2,1,0:T(8,128)(2,1)}), bf16[8,64,512]{2,1,0:T(8,128)(2,1)S(1)}, u32[]{:S(2)}, u32[]{:S(2)}) %all-to-all-start.1) | async-done | bytes 524320 | tf_op jit(solution)/shard_map/all_to_all | solution.py:65
  395.8 3.5 all-to-all-start.2
  399.3 0.9 copy.47
  400.2 24.6 %all-to-all-done.2 = bf16[8,64,512]{2,1,0:T(8,128)(2,1)S(1)} async-done(((bf16[8,64,512]{2,1,0:T(8,128)(2,1)}), bf16[8,64,512]{2,1,0:T(8,128)(2,1)S(1)}, u32[]{:S(2)}, u32[]{:S(2)}) %all-to-all-start.2) | async-done | bytes 524320 | tf_op jit(solution)/shard_map/all_to_all | solution.py:66
  424.8 2.1 pad_maximum_fusion
  426.9 2.1 add_convert_fusion
  (32 shorter events, 0.2 us)
Async XLA Ops:
  7.2 10.8 %copy-start = (bf16[512,2048]{1,0:T(8,128)(2,1)S(1)}, bf16[512,2048]{1,0:T(8,128)(2,1)}, u32[]{:S(2)}) copy-start(bf16[512,2048]{1,0:T(8,128)(2,1)} %param.19) | copy-start | bytes 6291460
  7.2 65.9 %reduce-scatter.3.cloned.1.call-start = ((), (), s32[]{:S(2)}) async-start(), calls=%async_computation.5 | async-start | bytes 2621440 | tf_op jit(solution)/shard_map/reduce_scatter | solution.py:73
  10.9 4.1 copy-start.4
  18.0 2.8 copy-start.11
  18.0 55.1 %copy-start.6 = (bf16[512,512]{1,0:T(8,128)(2,1)S(1)}, bf16[512,512]{1,0:T(8,128)(2,1)}, u32[]{:S(2)}) copy-start(bf16[512,512]{1,0:T(8,128)(2,1)} %param.17) | copy-start | bytes 1572868
  20.6 56.6 %copy-start.8 = (bf16[2048,16]{0,1:T(8,128)(2,1)S(1)}, bf16[2048,16]{0,1:T(8,128)(2,1)}, u32[]{:S(2)}) copy-start(bf16[2048,16]{0,1:T(8,128)(2,1)} %param.23) | copy-start | bytes 196612
  20.6 56.6 %copy-start.9 = (bf16[2048,16]{0,1:T(8,128)(2,1)S(1)}, bf16[2048,16]{0,1:T(8,128)(2,1)}, u32[]{:S(2)}) copy-start(bf16[2048,16]{0,1:T(8,128)(2,1)} %param.24) | copy-start | bytes 196612
  20.7 56.6 %copy-start.12 = (bf16[128,16]{0,1:T(8,128)(2,1)S(1)}, bf16[128,16]{0,1:T(8,128)(2,1)}, u32[]{:S(2)}) copy-start(bf16[128,16]{0,1:T(8,128)(2,1)} %param.22) | copy-start | bytes 12292
  20.7 106.0 %all-gather.4.cloned.1.call-start = ((), (), s32[]{:S(2)}) async-start(), calls=%async_computation.6 | async-start | bytes 2621440 | tf_op jit(solution)/shard_map/all_gather | solution.py:78
  76.2 114.6 %copy-start.10 = (f32[2048]{0:T(1024)S(1)}, f32[2048]{0:T(1024)}, u32[]{:S(2)}) copy-start(f32[2048]{0:T(1024)} %param.20) | copy-start | bytes 24580
  77.2 188.1 %all-gather.6.cloned.1.call-start = ((), (), s32[]{:S(2)}) async-start(), calls=%async_computation.7 | async-start | bytes 9052160 | tf_op jit(solution)/shard_map/all_gather | solution.py:101
  78.0 277.0 %all-gather.8.cloned.1.call-start = ((), (), s32[]{:S(2)}) async-start(), calls=%async_computation.8 | async-start | bytes 4259840 | tf_op jit(solution)/shard_map/all_gather | solution.py:105
  78.6 348.3 %reduce-scatter.5.cloned.1.call-start = ((), (), s32[]{:S(2)}) async-start(), calls=%async_computation.9 | async-start | bytes 2621440 | tf_op jit(solution)/shard_map/reduce_scatter | solution.py:109
  188.9 1.3 copy-start.1
  190.3 4.1 copy-start.7
  193.0 1.3 copy-start.2
  275.9 86.5 %copy-start.3 = (bf16[512,512]{1,0:T(8,128)(2,1)S(1)}, bf16[512,512]{1,0:T(8,128)(2,1)}, u32[]{:S(2)}) copy-start(bf16[512,512]{1,0:T(8,128)(2,1)} %param.15) | copy-start | bytes 1572868
  275.9 86.5 %copy-start.13 = (s32[1,8]{1,0:T(1,128)S(1)}, s32[1,8]{1,0:T(1,128)}, u32[]{:S(2)}) copy-start(s32[1,8]{1,0:T(1,128)} %param.27) | copy-start | bytes 100
  362.3 4.9 %copy-start.5 = (bf16[512,512]{1,0:T(8,128)(2,1)S(1)}, bf16[512,512]{1,0:T(8,128)(2,1)}, u32[]{:S(2)}) copy-start(bf16[512,512]{1,0:T(8,128)(2,1)} %param.16) | copy-start | bytes 1572868
  363.7 32.1 %all-to-all-start.1 = ((bf16[8,64,512]{2,1,0:T(8,128)(2,1)}), bf16[8,64,512]{2,1,0:T(8,128)(2,1)S(1)}, u32[]{:S(2)}, u32[]{:S(2)}) async-start(bf16[8,64,512]{2,1,0:T(8,128)(2,1)} %copy.38), calls=%async_computation.3 | async-start | bytes 1048576 | tf_op jit(solution)/shard_map/all_to_all | solution.py:65
  395.8 28.9 %all-to-all-start.2 = ((bf16[8,64,512]{2,1,0:T(8,128)(2,1)}), bf16[8,64,512]{2,1,0:T(8,128)(2,1)S(1)}, u32[]{:S(2)}, u32[]{:S(2)}) async-start(bf16[8,64,512]{2,1,0:T(8,128)(2,1)} %copy.41), calls=%async_computation.4 | async-start | bytes 1048576 | tf_op jit(solution)/shard_map/all_to_all | solution.py:66
Sparse Core Ops, SparseCore 0:
  20.8 52.2 reduce-scatter.2
  77.3 49.2 all-gather.3
  131.0 134.2 all-gather.5
  268.7 86.1 all-gather.7
  362.5 57.5 reduce-scatter.4
where the time goes:
time: 436 us
  waiting for transfers between devices  302 us (69%)
  blocking collectives  62.3 us (14%)
  matrix products  26.7 us (6%)
  other arithmetic  15.6 us (4%)
  between operations  14.1 us (3%)
  local copies, waits for them, and re-layouts  7.92 us (2%)
  starting transfers between devices  7.15 us (2%)
    all_gather x1, waiting for transfers between devices, body(): down_full = lax.all_gather(down_weight, 'req', axis=0, tiled=True)  79.1 us
    all_gather x1, waiting for transfers between devices, body(): lax.all_gather(stacked, 'req', axis=2, tiled=True)  70 us
    all_to_all x1, blocking collectives, body(): lax.all_to_all(whole_rows, 'req', split_axis=0, concat_axis=0, tiled=True)  62.3 us
    reduce_scatter x1, waiting for transfers between devices, body(): lax.psum_scatter(partial_value, 'dec', scatter_dimension=1, tiled=True)  52.3 us
    all_gather x1, waiting for transfers between devices, body(): whole_rows = lax.all_gather(permuted, 'dec', axis=1, tiled=True)  48 us
    all_to_all x1, waiting for transfers between devices, body(): lax.all_to_all(ordered_keys, 'dec', split_axis=0, concat_axis=2, tiled=True)  27.2 us
    all_to_all x1, waiting for transfers between devices, body(): lax.all_to_all(ordered_values, 'dec', split_axis=0, concat_axis=2, tiled=...  24.6 us
    dot_general x1, matrix products, body(): jnp.einsum('md,gdc->gmc', operand, lax.all_gather(stacked, 'req', axis=2,...  10.6 us
  transfers between devices with their start and end apart: 7, of which 6 were waited for; matrix products, arithmetic and copies ran while one was open for 5% of the time, Pallas kernels for 0%

commit v1 on v0

--- a/solution.py
+++ b/solution.py
@@ -98,7 +98,9 @@
     projected = jnp.einsum(
         "md,gdc->gmc",
         operand,
-        lax.all_gather(stacked, "req", axis=2, tiled=True),
+        jnp.concatenate(
+            lax.all_to_all(jnp.stack([stacked] * lax.axis_size("req")), "req", 0, 0), axis=2
+        ),
         preferred_element_type=jnp.float32,
     )
     hidden_units = (jax.nn.gelu(projected[0]) * projected[1]).astype(jnp.bfloat16)

time: 436 us -> 538 us (1.23)
  waiting for transfers between devices: 302 us -> 437 us
  blocking collectives: 62.3 us -> 0 us
  starting transfers between devices: 7.15 us -> 26.7 us
  local copies, waits for them, and re-layouts: 7.92 us -> 18.6 us
    all_to_all x0 -> x2, waiting for transfers between devices: none -> 151 us  [the longest x1 102 us: body(): lax.all_to_all(jnp.stack([stacked] * lax.axis_size('req')), 'req', 0, 0)]
    all_gather x1 -> x0, waiting for transfers between devices: 70 us -> none  [body(): lax.all_gather(stacked, 'req', axis=2, tiled=True)]
    all_to_all x1 -> x0, blocking collectives: 62.3 us -> none  [body(): lax.all_to_all(whole_rows, 'req', split_axis=0, concat_axis=0, tiled=True)]
    all_gather x1, waiting for transfers between devices: 79.1 us -> 132 us  [body(): down_full = lax.all_gather(down_weight, 'req', axis=0, tiled=True)]
    all_to_all x0 -> x2, starting transfers between devices: none -> 19.4 us  [the longest x1 11.9 us: body(): lax.all_to_all(whole_rows, 'req', split_axis=0, concat_axis=0, tiled=True)]
    reshape x0 -> x1, local copies, waits for them, and re-layouts: none -> 7.79 us  [body(): jnp.concatenate(lax.all_to_all(jnp.stack([stacked] * lax.axis_size('req')...]
  transfers between devices with their start and end apart: 7 -> 8, of which waited for: 6 -> 7; matrix products, arithmetic and copies ran while one was open for 5% -> 5% of each run, Pallas kernels for 0% -> 0%
where the time goes in v1:
time: 538 us
  waiting for transfers between devices  437 us (81%)
  starting transfers between devices  26.7 us (5%)
  matrix products  26.5 us (5%)
  local copies, waits for them, and re-layouts  18.6 us (3%)
  between operations  15.5 us (3%)
  other arithmetic  13.4 us (2%)
    all_gather x1, waiting for transfers between devices, body(): down_full = lax.all_gather(down_weight, 'req', axis=0, tiled=True)  132 us
    all_to_all x1, waiting for transfers between devices, body(): lax.all_to_all(jnp.stack([stacked] * lax.axis_size('req')), 'req', 0, 0)  102 us
    reduce_scatter x1, waiting for transfers between devices, body(): lax.psum_scatter(partial_value, 'dec', scatter_dimension=1, tiled=True)  52.3 us
    all_gather x1, waiting for transfers between devices, body(): whole_rows = lax.all_gather(permuted, 'dec', axis=1, tiled=True)  49.5 us
    all_to_all x1, waiting for transfers between devices, body(): lax.all_to_all(whole_rows, 'req', split_axis=0, concat_axis=0, tiled=True)  49.4 us
    all_to_all x1, waiting for transfers between devices, body(): lax.all_to_all(ordered_keys, 'dec', split_axis=0, concat_axis=2, tiled=True)  27.2 us
    all_to_all x1, waiting for transfers between devices, body(): lax.all_to_all(ordered_values, 'dec', split_axis=0, concat_axis=2, tiled=...  24.6 us
    all_to_all x1, starting transfers between devices, body(): lax.all_to_all(whole_rows, 'req', split_axis=0, concat_axis=0, tiled=True)  11.9 us
  transfers between devices with their start and end apart: 8, of which 7 were waited for; matrix products, arithmetic and copies ran while one was open for 5% of the time, Pallas kernels for 0%

profile of v1, /device:TPU:1, one launch (start us, length us, event | category | flops | bytes accessed | tf_op | source)
XLA Modules:
  0.0 537.8 jit_solution(3814338849770487057)
XLA Ops:
  8.0 0.0 copy-start
  8.0 0.0 reduce-scatter.3.cloned.1.call-start
  8.1 0.8 broadcast_compare_fusion
  8.9 1.0 fusion.26
  9.9 1.9 fusion.27
  11.8 4.1 fusion.46
  15.9 0.2 copy.45
  16.1 2.6 fusion.19
  18.8 0.0 copy-start.7
  18.8 2.6 convolution_convert_fusion.1
  21.4 0.0 reduce-scatter.3.cloned.1.call-update
  21.5 0.0 all-gather.3.cloned.1.call-start
  21.6 52.3 %reduce-scatter.3.cloned.1.call-done = bf16[512,512]{1,0:T(8,128)(2,1)} async-done(((bf16[512,2048]{1,0:T(8,128)(2,1)}), bf16[512,512]{1,0:T(8,128)(2,1)}) %reduce-scatter.3.cloned.1.call-update) | async-done | bytes 524304 | tf_op jit(solution)/shard_map/reduce_scatter | solution.py:73
  73.9 1.2 add_convert_fusion.1
  75.1 2.0 gather_fusion
  77.1 0.9 broadcast_select_fusion
  78.0 0.0 all-gather.3.cloned.1.call-update
  78.0 49.5 %all-gather.3.cloned.1.call-done = bf16[512,2048]{1,0:T(8,128)(2,1)} async-done(((bf16[512,512]{1,0:T(8,128)(2,1)}), bf16[512,2048]{1,0:T(8,128)(2,1)}) %all-gather.3.cloned.1.call-update) | async-done | bytes 2097168 | tf_op jit(solution)/shard_map/all_gather | solution.py:78
  127.5 11.9 %all-to-all-start = ((bf16[64,8,2048]{2,1,0:T(8,128)(2,1)}), bf16[64,8,2048]{2,1,0:T(8,128)(2,1)S(1)}, u32[]{:S(2)}, u32[]{:S(2)}) async-start(bf16[64,8,2048]{2,1,0:T(8,128)(2,1)} %bitcast.75), calls=%async_computation.1 | async-start | bytes 4194304 | tf_op jit(solution)/shard_map/all_to_all | solution.py:79
  139.5 49.4 %all-to-all-done = bf16[64,8,2048]{2,1,0:T(8,128)(2,1)S(1)} async-done(((bf16[64,8,2048]{2,1,0:T(8,128)(2,1)}), bf16[64,8,2048]{2,1,0:T(8,128)(2,1)S(1)}, u32[]{:S(2)}, u32[]{:S(2)}) %all-to-all-start) | async-done | bytes 2097184 | tf_op jit(solution)/shard_map/all_to_all | solution.py:79
  188.9 4.1 stack.11
  193.0 7.5 %all-to-all-start.1 = ((bf16[64,2,2176,16]{2,3,1,0:T(8,128)(2,1)}), bf16[64,2,2176,16]{2,3,1,0:T(8,128)(2,1)}, u32[]{:S(2)}, u32[]{:S(2)}) async-start(bf16[64,2,2176,16]{2,3,1,0:T(8,128)(2,1)} %stack.11), calls=%async_computation.2 | async-start | bytes 17825792 | tf_op jit(solution)/shard_map/all_to_all | solution.py:102
  200.5 0.0 all-gather.5.cloned.1.call-start
  200.6 0.5 all-gather.5.cloned.1.call-update
  201.1 0.2 reduce-scatter.5.cloned.1.call-start
  201.3 0.5 multiply_reduce_fusion
  201.8 0.1 rsqrt.12
  202.0 0.5 multiply_convert_fusion
  202.5 1.4 copy-done.3
  203.9 0.8 convolution_convert_fusion.4
  204.8 0.1 copy.37
  204.9 102.0 %all-to-all-done.1 = bf16[64,2,2176,16]{2,3,1,0:T(8,128)(2,1)} async-done(((bf16[64,2,2176,16]{2,3,1,0:T(8,128)(2,1)}), bf16[64,2,2176,16]{2,3,1,0:T(8,128)(2,1)}, u32[]{:S(2)}, u32[]{:S(2)}) %all-to-all-start.1) | async-done | bytes 8912928 | tf_op jit(solution)/shard_map/all_to_all | solution.py:102
  306.9 7.8 %copy.36 = bf16[2,2176,64,16]{1,3,2,0:T(8,128)(2,1)} copy(bf16[2,2176,64,16]{1,3,0,2:T(8,128)(2,1)} %bitcast.10) | data formatting | bytes 17825792 | tf_op jit(solution)/shard_map/reshape | solution.py:101
  314.7 10.3 %fusion.5 = f32[2,512,1024]{1,2,0:T(8,128)} fusion(bf16[2,2176,1024]{1,2,0:T(8,128)(2,1)} %bitcast.73, bf16[512,128]{1,0:T(8,128)(2,1)S(1)} %copy.37, bf16[512,2048]{1,0:T(8,128)(2,1)S(1)} %copy-done.4), kind=kOutput, calls=%fused_computation.15 | convolution fusion | flops 4567859200 | bytes 15335424 | tf_op jit(solution)/shard_map/md,gdc->gmc/dot_general | solution.py:98
  325.0 131.6 %all-gather.5.cloned.1.call-done = bf16[1024,2048]{1,0:T(8,128)(2,1)} async-done(((bf16[16,2048]{1,0:T(8,128)(2,1)}), bf16[1024,2048]{1,0:T(8,128)(2,1)}) %all-gather.5.cloned.1.call-update) | async-done | bytes 4194320 | tf_op jit(solution)/shard_map/all_gather | solution.py:107
  456.6 7.4 %convolution_convert_fusion = bf16[512,2048]{1,0:T(8,128)(2,1)} fusion(bf16[1024,2048]{1,0:T(8,128)(2,1)} %all-gather.5.cloned.1.call-done, f32[2,512,1024]{1,2,0:T(8,128)} %fusion.5), kind=kOutput, calls=%fused_computation.9 | convolution fusion | flops 2153775104 | bytes 10485760 | tf_op jit(solution)/shard_map/dot_general | solution.py:108
  464.0 0.0 reduce-scatter.5.cloned.1.call-update
  464.0 0.4 convolution_convert_fusion.3
  464.4 0.9 copy.39
  465.4 3.5 all-to-all-start.2
  468.9 0.4 convolution_convert_fusion.2
  469.3 0.9 copy.42
  470.2 27.2 %all-to-all-done.2 = bf16[8,64,512]{2,1,0:T(8,128)(2,1)S(1)} async-done(((bf16[8,64,512]{2,1,0:T(8,128)(2,1)}), bf16[8,64,512]{2,1,0:T(8,128)(2,1)S(1)}, u32[]{:S(2)}, u32[]{:S(2)}) %all-to-all-start.2) | async-done | bytes 524320 | tf_op jit(solution)/shard_map/all_to_all | solution.py:65
  497.5 3.5 all-to-all-start.3
  501.0 0.9 copy.48
  501.8 24.6 %all-to-all-done.3 = bf16[8,64,512]{2,1,0:T(8,128)(2,1)S(1)} async-done(((bf16[8,64,512]{2,1,0:T(8,128)(2,1)}), bf16[8,64,512]{2,1,0:T(8,128)(2,1)S(1)}, u32[]{:S(2)}, u32[]{:S(2)}) %all-to-all-start.3) | async-done | bytes 524320 | tf_op jit(solution)/shard_map/all_to_all | solution.py:66
  526.5 2.1 pad_maximum_fusion
  528.6 2.1 add_convert_fusion
  (36 shorter events, 0.2 us)
Async XLA Ops:
  8.0 10.8 %copy-start = (bf16[512,2048]{1,0:T(8,128)(2,1)S(1)}, bf16[512,2048]{1,0:T(8,128)(2,1)}, u32[]{:S(2)}) copy-start(bf16[512,2048]{1,0:T(8,128)(2,1)} %param.19) | copy-start | bytes 6291460
  8.0 65.9 %reduce-scatter.3.cloned.1.call-start = ((), (), s32[]{:S(2)}) async-start(), calls=%async_computation.6 | async-start | bytes 2621440 | tf_op jit(solution)/shard_map/reduce_scatter | solution.py:73
  11.8 4.1 copy-start.6
  18.8 2.7 copy-start.12
  18.8 55.1 %copy-start.7 = (bf16[512,512]{1,0:T(8,128)(2,1)S(1)}, bf16[512,512]{1,0:T(8,128)(2,1)}, u32[]{:S(2)}) copy-start(bf16[512,512]{1,0:T(8,128)(2,1)} %param.17) | copy-start | bytes 1572868
  21.5 106.1 %all-gather.3.cloned.1.call-start = ((), (), s32[]{:S(2)}) async-start(), calls=%async_computation.7 | async-start | bytes 2621440 | tf_op jit(solution)/shard_map/all_gather | solution.py:78
  75.1 64.4 %copy-start.9 = (bf16[2048,16]{0,1:T(8,128)(2,1)S(1)}, bf16[2048,16]{0,1:T(8,128)(2,1)}, u32[]{:S(2)}) copy-start(bf16[2048,16]{0,1:T(8,128)(2,1)} %param.23) | copy-start | bytes 196612
  75.1 64.4 %copy-start.10 = (bf16[2048,16]{0,1:T(8,128)(2,1)S(1)}, bf16[2048,16]{0,1:T(8,128)(2,1)}, u32[]{:S(2)}) copy-start(bf16[2048,16]{0,1:T(8,128)(2,1)} %param.24) | copy-start | bytes 196612
  75.1 64.4 %copy-start.13 = (bf16[128,16]{0,1:T(8,128)(2,1)S(1)}, bf16[128,16]{0,1:T(8,128)(2,1)}, u32[]{:S(2)}) copy-start(bf16[128,16]{0,1:T(8,128)(2,1)} %param.22) | copy-start | bytes 12292
  127.5 61.4 %all-to-all-start = ((bf16[64,8,2048]{2,1,0:T(8,128)(2,1)}), bf16[64,8,2048]{2,1,0:T(8,128)(2,1)S(1)}, u32[]{:S(2)}, u32[]{:S(2)}) async-start(bf16[64,8,2048]{2,1,0:T(8,128)(2,1)} %bitcast.75), calls=%async_computation.1 | async-start | bytes 4194304 | tf_op jit(solution)/shard_map/all_to_all | solution.py:79
  188.9 13.0 %copy-start.2 = (bf16[64,8,2048]{2,1,0:T(8,128)(2,1)}, bf16[64,8,2048]{2,1,0:T(8,128)(2,1)S(1)}, u32[]{:S(2)}) copy-start(bf16[64,8,2048]{2,1,0:T(8,128)(2,1)S(1)} %all-to-all-done) | copy-start | bytes 6291460
  193.0 8.9 %copy-start.11 = (f32[2048]{0:T(1024)S(1)}, f32[2048]{0:T(1024)}, u32[]{:S(2)}) copy-start(f32[2048]{0:T(1024)} %param.20) | copy-start | bytes 24580
  193.0 113.8 %all-to-all-start.1 = ((bf16[64,2,2176,16]{2,3,1,0:T(8,128)(2,1)}), bf16[64,2,2176,16]{2,3,1,0:T(8,128)(2,1)}, u32[]{:S(2)}, u32[]{:S(2)}) async-start(bf16[64,2,2176,16]{2,3,1,0:T(8,128)(2,1)} %stack.11), calls=%async_computation.2 | async-start | bytes 17825792 | tf_op jit(solution)/shard_map/all_to_all | solution.py:102
  200.5 3.4 copy-start.8
  200.5 256.1 %all-gather.5.cloned.1.call-start = ((), (), s32[]{:S(2)}) async-start(), calls=%async_computation.8 | async-start | bytes 4259840 | tf_op jit(solution)/shard_map/all_gather | solution.py:107
  201.1 327.5 %reduce-scatter.5.cloned.1.call-start = ((), (), s32[]{:S(2)}) async-start(), calls=%async_computation.9 | async-start | bytes 2621440 | tf_op jit(solution)/shard_map/reduce_scatter | solution.py:111
  202.5 1.4 copy-start.3
  306.9 7.8 %copy-start.4 = (bf16[512,2048]{1,0:T(8,128)(2,1)S(1)}, bf16[512,2048]{1,0:T(8,128)(2,1)}, u32[]{:S(2)}) copy-start(bf16[512,2048]{1,0:T(8,128)(2,1)} %copy-done.3) | copy-start | bytes 6291460
  325.0 139.0 %copy-start.5 = (bf16[512,512]{1,0:T(8,128)(2,1)S(1)}, bf16[512,512]{1,0:T(8,128)(2,1)}, u32[]{:S(2)}) copy-start(bf16[512,512]{1,0:T(8,128)(2,1)} %param.15) | copy-start | bytes 1572868
  325.0 139.1 %copy-start.14 = (s32[1,8]{1,0:T(1,128)S(1)}, s32[1,8]{1,0:T(1,128)}, u32[]{:S(2)}) copy-start(s32[1,8]{1,0:T(1,128)} %param.27) | copy-start | bytes 100
  465.4 32.1 %all-to-all-start.2 = ((bf16[8,64,512]{2,1,0:T(8,128)(2,1)}), bf16[8,64,512]{2,1,0:T(8,128)(2,1)S(1)}, u32[]{:S(2)}, u32[]{:S(2)}) async-start(bf16[8,64,512]{2,1,0:T(8,128)(2,1)} %copy.39), calls=%async_computation.4 | async-start | bytes 1048576 | tf_op jit(solution)/shard_map/all_to_all | solution.py:65
  468.9 61.8 %copy-start.1 = (bf16[512,2048]{1,0:T(8,128)(2,1)S(1)}, bf16[512,2048]{1,0:T(8,128)(2,1)}, u32[]{:S(2)}) copy-start(bf16[512,2048]{1,0:T(8,128)(2,1)} %param.19) | copy-start | bytes 6291460
  497.5 28.9 %all-to-all-start.3 = ((bf16[8,64,512]{2,1,0:T(8,128)(2,1)}), bf16[8,64,512]{2,1,0:T(8,128)(2,1)S(1)}, u32[]{:S(2)}, u32[]{:S(2)}) async-start(bf16[8,64,512]{2,1,0:T(8,128)(2,1)} %copy.42), calls=%async_computation.5 | async-start | bytes 1048576 | tf_op jit(solution)/shard_map/all_to_all | solution.py:66
Sparse Core Ops, SparseCore 0:
  21.6 52.2 reduce-scatter.2
  78.2 49.2 all-gather.2
  464.1 57.5 reduce-scatter.4
Sparse Core Ops, SparseCore 1:
  204.6 251.9 all-gather.4
